TPU v7x, 32 devices: a whole 2x2x4 slice. The times are simulated.
32 devices in a mesh: dp: 4 (over y, x), section: 2 (over core), tensor: 4 (over z).
Axes of the slice: x: 2, y: 2, z: 4, core: 2. Of those that a mesh axis runs over, the one named last changes fastest.
Arguments:
- stored: bfloat16 [2, 2, 256, 8192], P('section', None, 'dp', 'tensor'), may hold values from -6 to 6
- cotangent: bfloat16 [2, 32, 8192], P(None, None, 'tensor'), may hold values from -12 to 12
- positions: int32 [2, 32], replicated, may hold values from 128 to 255, as said below
- lengths: int32 [2], replicated, may hold values from 128 to 256, as said below
- norm_gain: float32 [2, 8192], P('section'), may hold values from 0.5 to 1.5
- w_query: bfloat16 [2, 8192, 8192], P('section', None, 'tensor')
- w_key: bfloat16 [2, 8192, 1024], P('section', None, 'tensor')
- w_value: bfloat16 [2, 8192, 1024], P('section', None, 'tensor'), may hold values from -0.0625 to 0.0625
- w_out: bfloat16 [2, 8192, 8192], P('section', 'tensor', 'dp'), may hold values from -0.0625 to 0.0625
Outputs:
- input_grads: float32 [2, 2, 256, 8192], P('section', None, 'dp', 'tensor')
Inputs may be any that keep to these rules, and one draw needn't show every extreme that they name: In each sequence the response positions are distinct, rise along the last dimension, lie in the last 128 positions, and the last one is 255. `lengths`: some sequence has length 256.
All inputs are finite; a program needn't handle non-finite values.
Results may differ from a plain program's by a relative error of at most 0.017.
Values may be sent and summed in bfloat16 or wider, within the bound.
A program may use at most 256 MiB of HBM per device.

v0:
```python
import math
import jax
import jax.numpy as jnp
from jax import lax
from jax.sharding import PartitionSpec as P

HD = 128
EPS = 1e-05
THETA = 500000.0


def passed_along(value, axis, steps):
    count = lax.axis_size(axis)
    leading, last = (max(0, -steps), min(count, count - steps))
    return lax.ppermute(value, axis, [(source, source + steps) for source in range(leading, last)])


def angle_tables(row_places):
    half_dim = HD // 2
    frequency = THETA ** (-(jnp.arange(half_dim, dtype=jnp.float32) * 2.0) / HD)
    angles = row_places[:, None] * frequency[None, :]
    cosine = jnp.concatenate([jnp.cos(angles), jnp.cos(angles)], -1)[:, None, :]
    sine_table = jnp.concatenate([jnp.sin(angles), jnp.sin(angles)], -1)[:, None, :]
    return (cosine, sine_table)


def turn_half(values):
    half_dim = values.shape[-1] // 2
    return jnp.concatenate([-values[..., half_dim:], values[..., :half_dim]], -1)


def rotate(values, cosine, sine_table):
    return values * cosine + turn_half(values) * sine_table


def unrotate(values, cosine, sine_table):
    return values * cosine - turn_half(values * sine_table)


def layer_grad(own_input, own_upstream, seq_lengths, gain, w_query, w_key, w_value, w_out):
    batch, rows, width_dev = own_input.shape
    kv_dev = w_key.shape[1] // HD
    q_dev = w_query.shape[1] // HD
    group = q_dev // kv_dev
    scale = 1.0 / math.sqrt(HD)
    x_whole, g_whole = (
        lax.all_gather(own_input, "tensor", axis=2, tiled=True),
        lax.all_gather(own_upstream, "tensor", axis=2, tiled=True),
    )
    width = x_whole.shape[2]
    x_full = x_whole.astype(jnp.float32)
    inv_rms = lax.rsqrt(jnp.mean(x_full * x_full, -1, keepdims=True) + EPS)
    normed = (x_full * inv_rms * gain).astype(jnp.bfloat16)
    first_row = lax.axis_index("dp") * rows
    query_ids = first_row + jnp.arange(rows, dtype=jnp.int32)
    cosine, sine_table = angle_tables(query_ids.astype(jnp.float32))
    queries = jnp.einsum(
        "bpd,dc->bpc", normed, w_query, preferred_element_type=jnp.float32
    ).reshape(batch, rows, q_dev, HD)
    keys = jnp.einsum("bpd,dc->bpc", normed, w_key, preferred_element_type=jnp.float32).reshape(
        batch, rows, kv_dev, HD
    )
    values = jnp.einsum("bpd,dc->bpc", normed, w_value, preferred_element_type=jnp.float32).reshape(
        batch, rows, kv_dev, HD
    )
    q_rot = rotate(queries, cosine, sine_table).astype(jnp.bfloat16)
    k_rot = rotate(keys, cosine, sine_table).astype(jnp.bfloat16)
    values_b = values.astype(jnp.bfloat16)
    grad_out = jnp.einsum("bpd,cd->bpc", g_whole, w_out, preferred_element_type=jnp.float32).astype(
        jnp.bfloat16
    )
    all_keys, all_values = (
        lax.all_gather(k_rot, "dp", axis=1, tiled=True),
        lax.all_gather(values_b, "dp", axis=1, tiled=True),
    )
    length = all_keys.shape[1]
    q_five = q_rot.reshape(batch, rows, kv_dev, group, HD)
    o_five = grad_out.reshape(batch, rows, kv_dev, group, HD)
    key_ids = jnp.arange(length, dtype=jnp.int32)
    causal = key_ids[None, None, :] <= query_ids[None, :, None]
    start_pos = length - seq_lengths
    inside = (key_ids[None, None, :] >= start_pos[:, None, None]) | (
        key_ids[None, None, :] == query_ids[None, :, None]
    )
    allowed = (causal & inside)[:, None, None, :, :]
    scores = (
        jnp.einsum("bpkgd,bjkd->bkgpj", q_five, all_keys, preferred_element_type=jnp.float32)
        * scale
    )
    masked = jnp.where(allowed, scores, -1e30)
    highest = jnp.max(masked, -1, keepdims=True)
    expo_terms = jnp.where(allowed, jnp.exp(masked - highest), 0.0)
    probs = expo_terms / jnp.sum(expo_terms, -1, keepdims=True)
    grad_probs = jnp.einsum(
        "bpkgd,bjkd->bkgpj", o_five, all_values, preferred_element_type=jnp.float32
    )
    row_dot = jnp.sum(probs * grad_probs, -1, keepdims=True)
    grad_scores = (probs * (grad_probs - row_dot) * scale).astype(jnp.bfloat16)
    probs_b = probs.astype(jnp.bfloat16)
    grad_qr = jnp.einsum(
        "bkgpj,bjkd->bpkgd", grad_scores, all_keys, preferred_element_type=jnp.float32
    )
    key_terms = jnp.einsum(
        "bkgpj,bpkgd->bjkd", grad_scores, q_five, preferred_element_type=jnp.float32
    )
    value_terms = jnp.einsum(
        "bkgpj,bpkgd->bjkd", probs_b, o_five, preferred_element_type=jnp.float32
    )
    grad_kr, grad_vr = (
        lax.psum_scatter(
            key_terms.astype(jnp.bfloat16), "dp", scatter_dimension=1, tiled=True
        ).astype(jnp.float32),
        lax.psum_scatter(
            value_terms.astype(jnp.bfloat16), "dp", scatter_dimension=1, tiled=True
        ).astype(jnp.float32),
    )
    grad_q = (
        unrotate(grad_qr.reshape(batch, rows, q_dev, HD), cosine, sine_table)
        .astype(jnp.bfloat16)
        .reshape(batch, rows, q_dev * HD)
    )
    grad_k = (
        unrotate(grad_kr, cosine, sine_table).astype(jnp.bfloat16).reshape(batch, rows, kv_dev * HD)
    )
    grad_v = grad_vr.astype(jnp.bfloat16).reshape(batch, rows, kv_dev * HD)
    partial_term = jnp.einsum("bpc,dc->bpd", grad_q, w_query, preferred_element_type=jnp.float32)
    partial_term = partial_term + jnp.einsum(
        "bpc,dc->bpd", grad_k, w_key, preferred_element_type=jnp.float32
    )
    partial_term = partial_term + jnp.einsum(
        "bpc,dc->bpd", grad_v, w_value, preferred_element_type=jnp.float32
    )
    summed = lax.psum(partial_term.astype(jnp.bfloat16), "tensor").astype(jnp.float32)
    stat = jnp.sum(x_full * gain * summed, -1, keepdims=True)
    whole_grad = (
        g_whole.astype(jnp.float32) + inv_rms * gain * summed - x_full * inv_rms**3 * stat / width
    )
    return lax.dynamic_slice_in_dim(whole_grad, lax.axis_index("tensor") * width_dev, width_dev, 2)


def on_device(stored, cotangent, positions, lengths, norm_gain, w_query, w_key, w_value, w_out):
    own_input = stored[0]
    gain = norm_gain[0]
    wq_layer = w_query[0]
    wk_layer = w_key[0]
    wv_layer = w_value[0]
    wo_layer = lax.all_gather(w_out[0], "dp", axis=1, tiled=True)
    seqs, rows, width_dev = own_input.shape
    section_id = lax.axis_index("section")
    row_ids = lax.axis_index("dp") * rows + jnp.arange(rows, dtype=jnp.int32)
    placed = (positions[:, None, :] == row_ids[None, :, None]).astype(jnp.bfloat16)
    from_loss = jnp.einsum(
        "spr,srd->spd", placed, cotangent, preferred_element_type=jnp.float32
    ).astype(jnp.bfloat16)

    def run_layer(input_part, upstream_part, length_part):
        return layer_grad(
            input_part, upstream_part, length_part, gain, wq_layer, wk_layer, wv_layer, wo_layer
        )

    first_in = jnp.where(section_id == 1, from_loss, jnp.zeros_like(from_loss))
    first_pass = run_layer(own_input, first_in, lengths)
    handed = passed_along(first_pass.astype(jnp.bfloat16), "section", -1)
    second_pass = run_layer(own_input, handed, lengths)
    result = jnp.where(section_id == 0, second_pass, first_pass)
    return result[None]


def solution(mesh):
    return jax.shard_map(
        on_device,
        mesh=mesh,
        in_specs=(
            P("section", None, "dp", "tensor"),
            P(None, None, "tensor"),
            P(),
            P(),
            P("section", None),
            P("section", None, "tensor"),
            P("section", None, "tensor"),
            P("section", None, "tensor"),
            P("section", "tensor", "dp"),
        ),
        out_specs=P("section", None, "dp", "tensor"),
        check_vma=False,
    )
```

profile of v0, /device:TPU:0, one launch (start us, length us, event | category | flops | bytes accessed | tf_op | source)
XLA Modules:
  0.0 914.5 jit_solution(1680415631563956756)
XLA Ops:
  7.5 2.0 fusion.50
  10.3 40.0 %copy.63 = bf16[2048,8192]{1,0:T(8,128)(2,1)} copy(bf16[2048,8192]{0,1:T(8,128)(2,1)} %bitcast.235) | data formatting | bytes 67108864 | tf_op jit(solution)/shard_map/bpd,dc->bpc/dot_general | solution.py:57
  50.3 6.4 copy.62
  56.7 6.4 copy.64
  64.9 2.3 fusion.33
  67.4 3.9 fusion.117
  71.5 10.4 %all_gather.23 = bf16[2,256,2,128]{3,1,2,0:T(8,128)(2,1)S(1)} all-gather(bf16[2,64,2,128]{3,1,2,0:T(8,128)(2,1)S(1)} %fusion.113), channel_id=1, replica_groups=mesh['dp'=4,'section'=2,'tensor'=4] {'dp'}, dimensions={1}, use_global_device_ids=true | all-gather | bytes 327680 | tf_op jit(solution)/shard_map/all_gather | solution.py:73
  81.9 1.5 convolution_convert_fusion.1
  83.4 9.6 %all_gather.24 = bf16[2,256,2,128]{3,1,2,0:T(8,128)(2,1)S(1)} all-gather(bf16[2,64,2,128]{3,1,2,0:T(8,128)(2,1)S(1)} %convolution_convert_fusion.1), channel_id=1, replica_groups=mesh['dp'=4,'section'=2,'tensor'=4] {'dp'}, dimensions={1}, use_global_device_ids=true | all-gather | bytes 327680 | tf_op jit(solution)/shard_map/all_gather | solution.py:74
  93.1 15.8 %fusion.115 = f32[2,64,16,128]{3,1,2,0:T(8,128)S(1)} fusion(bf16[16,128,8192,1]{2,1,0,3:T(8,128)(2,1)} %bitcast.236, bf16[1,2,64,8192]{3,2,1,0:T(8,128)(2,1)S(1)} %copy-done.2, f32[8192]{0:T(1024)S(1)} %bitcast.253, f32[2,64]{1,0:T(2,128)S(1)} %get-tuple-element.23), kind=kOutput, calls=%fused_computation.131 | convolution fusion | flops 4299161600 | bytes 36733440 | tf_op jit(solution)/shard_map/bpd,dc->bpc/dot_general | solution.py:57
  109.7 2.3 fusion.146
  112.0 3.8 fusion.143
  115.8 285.4 %all-gather.13.cloned.1.call-done = bf16[1,2048,8192]{2,1,0:T(8,128)(2,1)} async-done(((bf16[1,2048,2048]{2,1,0:T(8,128)(2,1)}), bf16[1,2048,8192]{2,1,0:T(8,128)(2,1)}) %all-gather.13.cloned.1.call-update) | async-done | bytes 33554448 | tf_op jit(solution)/shard_map/all_gather | solution.py:147
  401.2 16.4 %fusion.44 = bf16[2,64,2048]{2,1,0:T(8,128)(2,1)S(1)} fusion(bf16[2,64,8192]{2,1,0:T(8,128)(2,1)} %all-gather.7.cloned.1.call-done, bf16[1,2048,8192]{2,1,0:T(8,128)(2,1)} %all-gather.13.cloned.1.call-done), kind=kOutput, calls=%fused_computation.36 | convolution fusion | flops 4295229440 | bytes 36175872 | tf_op jit(solution)/shard_map/bpd,cd->bpc/dot_general | solution.py:69
  418.5 1.7 fusion.96
  420.2 15.5 %fusion.77 = f32[2,2,128,8,64]{2,4,3,1,0:T(8,128)} fusion(f32[2,2,256,64,8]{2,3,4,1,0:T(8,128)} %fusion.96, bf16[2,256,2,128]{3,1,2,0:T(8,128)(2,1)S(1)} %all_gather.23, f32[2,2,8,64,256]{4,3,2,1,0:T(8,128)} %get-tuple-element.29, f32[2,2,8,64]{3,2,1,0:T(8,128)S(1)} %get-tuple-element.28), kind=kOutput, calls=%fused_computation.86 | convolution fusion | flops 137890048 | bytes 5513216 | tf_op jit(solution)/shard_map/bkgpj,bjkd->bpkgd/dot_general | solution.py:100
  435.7 1.4 broadcast_multiply_fusion.2
  437.4 1.5 fusion.65
  438.9 1.8 copy.45
  441.3 1.7 slice_negate_fusion.1
  443.0 16.3 %fusion.66 = bf16[2,256,2,128]{3,1,2,0:T(8,128)(2,1)} fusion(bf16[2,64,2,8,128]{4,1,3,2,0:T(8,128)(2,1)} %bitcast.257, f32[2,2,256,64,8]{2,3,4,1,0:T(8,128)} %fusion.96, f32[2,2,8,64,256]{4,3,2,1,0:T(8,128)} %get-tuple-element.29, f32[2,2,8,64]{3,2,1,0:T(8,128)S(1)} %get-tuple-element.28), kind=kOutput, calls=%fused_computation.66 | convolution fusion | flops 138021120 | bytes 4988928 | tf_op jit(solution)/shard_map/bkgpj,bpkgd->bjkd/dot_general | solution.py:103
  459.4 24.7 %all-reduce.11.cloned.1.call-done = bf16[2,256,2,128]{3,2,0,1:T(2,128)(2,1)} async-done(((bf16[2,256,2,128]{3,2,0,1:T(2,128)(2,1)}), bf16[2,256,2,128]{3,2,0,1:T(2,128)(2,1)}) %all-reduce.11.cloned.1.call-update) | async-done | bytes 262160
  485.0 5.8 fusion.38
  490.8 20.3 %reduce-scatter.3.cloned.1.call-done = bf16[2,64,2,128]{3,1,2,0:T(8,128)(2,1)} async-done(((bf16[2,256,2,128]{3,1,2,0:T(8,128)(2,1)}), bf16[2,64,2,128]{3,1,2,0:T(8,128)(2,1)}) %reduce-scatter.3.cloned.1.call-update) | async-done | bytes 65552 | tf_op jit(solution)/shard_map/reduce_scatter | solution.py:110
  512.0 5.8 fusion.42
  517.8 19.2 %fusion.26 = bf16[2,64,8192]{2,1,0:T(8,128)(2,1)} fusion(f32[2,64,8192]{2,1,0:T(8,128)} %fusion.38, f32[2,64,8192]{2,1,0:T(8,128)} %fusion.42, bf16[1,8192,2048]{2,1,0:T(8,128)(2,1)} %param.14, f32[2,64,16,64]{3,1,2,0:T(8,128)} %get-tuple-element.12, f32[2,64,16,64]{3,1,2,0:T(8,128)} %get-tuple-element.11, f32[2,64,16,128]{3,1,2,0:T(8,128)S(1)} %bitcast.242, ...), kind=kOutput, calls=%fused_computation.16 | convolution fusion | flops 4299161600 | bytes 46170112 | tf_op jit(solution)/shard_map/bpc,dc->bpd/dot_general | solution.py:126
  537.1 86.2 %all-reduce.7.cloned.1.call-done = bf16[2,64,8192]{2,1,0:T(8,128)(2,1)} async-done(((bf16[2,64,8192]{2,1,0:T(8,128)(2,1)}), bf16[2,64,8192]{2,1,0:T(8,128)(2,1)}) %all-reduce.7.cloned.1.call-update) | async-done | bytes 2097168 | tf_op jit(solution)/shard_map/psum | solution.py:133
  623.4 2.2 convert_element_type.155
  625.6 2.0 convert_multiply_fusion.1
  627.6 3.4 fusion.144
  632.4 2.5 collective-permute-done
  636.0 44.6 %all-gather.9.cloned.1.call-done = bf16[2,64,8192]{2,1,0:T(8,128)(2,1)} async-done(((bf16[2,64,2048]{2,1,0:T(8,128)(2,1)}), bf16[2,64,8192]{2,1,0:T(8,128)(2,1)}) %all-gather.9.cloned.1.call-update) | async-done | bytes 2097168 | tf_op jit(solution)/shard_map/all_gather | solution.py:48
  680.6 16.4 %fusion.47 = bf16[2,64,2048]{2,1,0:T(8,128)(2,1)S(1)} fusion(bf16[2,64,8192]{2,1,0:T(8,128)(2,1)} %all-gather.9.cloned.1.call-done, bf16[1,2048,8192]{2,1,0:T(8,128)(2,1)} %all-gather.13.cloned.1.call-done), kind=kOutput, calls=%fused_computation.37 | convolution fusion | flops 4295229440 | bytes 36175872 | tf_op jit(solution)/shard_map/bpd,cd->bpc/dot_general | solution.py:69
  697.1 1.8 fusion.93
  698.9 1.5 fusion.63
  700.4 15.6 %fusion.79 = f32[2,2,128,8,64]{2,4,3,1,0:T(8,128)} fusion(f32[2,2,256,64,8]{2,3,4,1,0:T(8,128)} %fusion.93, bf16[2,256,2,128]{3,1,2,0:T(8,128)(2,1)S(1)} %copy-done.21, f32[2,2,8,64,256]{4,3,2,1,0:T(8,128)} %get-tuple-element.29, f32[2,2,8,64]{3,2,1,0:T(8,128)S(1)} %get-tuple-element.28), kind=kOutput, calls=%fused_computation.88 | convolution fusion | flops 137890048 | bytes 5513216 | tf_op jit(solution)/shard_map/bkgpj,bjkd->bpkgd/dot_general | solution.py:100
  716.0 1.3 broadcast_multiply_fusion.1
  717.3 1.8 copy.53
  719.2 1.8 slice_negate_fusion
  721.0 16.3 %fusion.64 = bf16[2,256,2,128]{3,1,2,0:T(8,128)(2,1)} fusion(bf16[2,64,2,8,128]{4,1,3,2,0:T(8,128)(2,1)} %bitcast.258, f32[2,2,256,64,8]{2,3,4,1,0:T(8,128)} %fusion.93, f32[2,2,8,64,256]{4,3,2,1,0:T(8,128)} %get-tuple-element.29, f32[2,2,8,64]{3,2,1,0:T(8,128)S(1)} %get-tuple-element.28), kind=kOutput, calls=%fused_computation.64 | convolution fusion | flops 138021120 | bytes 4988928 | tf_op jit(solution)/shard_map/bkgpj,bpkgd->bjkd/dot_general | solution.py:103
  737.6 23.7 %all-reduce.13.cloned.1.call-done = bf16[2,256,2,128]{3,2,0,1:T(2,128)(2,1)} async-done(((bf16[2,256,2,128]{3,2,0,1:T(2,128)(2,1)}), bf16[2,256,2,128]{3,2,0,1:T(2,128)(2,1)}) %all-reduce.13.cloned.1.call-update) | async-done | bytes 262160
  762.2 5.6 fusion.36
  767.9 20.6 %reduce-scatter.5.cloned.1.call-done = bf16[2,64,2,128]{3,1,2,0:T(8,128)(2,1)} async-done(((bf16[2,256,2,128]{3,1,2,0:T(8,128)(2,1)}), bf16[2,64,2,128]{3,1,2,0:T(8,128)(2,1)}) %reduce-scatter.5.cloned.1.call-update) | async-done | bytes 65552 | tf_op jit(solution)/shard_map/reduce_scatter | solution.py:110
  789.4 5.8 fusion.40
  795.2 19.3 %fusion.23 = bf16[2,64,8192]{2,1,0:T(8,128)(2,1)} fusion(f32[2,64,8192]{2,1,0:T(8,128)} %fusion.36, f32[2,64,8192]{2,1,0:T(8,128)} %fusion.40, bf16[1,8192,2048]{2,1,0:T(8,128)(2,1)} %param.14, f32[2,64,16,64]{3,1,2,0:T(8,128)} %get-tuple-element.10, f32[2,64,16,64]{3,1,2,0:T(8,128)} %get-tuple-element.9, f32[2,64,16,128]{3,1,2,0:T(8,128)S(1)} %bitcast.240, ...), kind=kOutput, calls=%fused_computation.15 | convolution fusion | flops 4299161600 | bytes 46170112 | tf_op jit(solution)/shard_map/bpc,dc->bpd/dot_general | solution.py:126
  814.6 86.3 %all-reduce.9.cloned.1.call-done = bf16[2,64,8192]{2,1,0:T(8,128)(2,1)} async-done(((bf16[2,64,8192]{2,1,0:T(8,128)(2,1)}), bf16[2,64,8192]{2,1,0:T(8,128)(2,1)}) %all-reduce.9.cloned.1.call-update) | async-done | bytes 2097168 | tf_op jit(solution)/shard_map/psum | solution.py:133
  900.8 2.2 convert_element_type.169
  904.3 3.1 fusion.70
  (97 shorter events, 13.8 us)
Async XLA Ops:
  6.5 1.0 copy-start
  6.5 58.4 %all-gather.11.cloned.1.call-start = ((), (), s32[]{:S(2)}) async-start(), calls=%async_computation.8 | async-start | bytes 2621440 | tf_op jit(solution)/shard_map/all_gather | solution.py:47
  7.3 108.6 %all-gather.7.cloned.1.call-start = ((), (), s32[]{:S(2)}) async-start(), calls=%async_computation.2 | async-start | bytes 2621440 | tf_op jit(solution)/shard_map/all_gather | solution.py:48
  9.5 391.7 %all-gather.13.cloned.1.call-start = ((), (), s32[]{:S(2)}) async-start(), calls=%async_computation.9 | async-start | bytes 41943040 | tf_op jit(solution)/shard_map/all_gather | solution.py:147
  10.2 473.9 %all-reduce.11.cloned.1.call-start = ((), (), s32[]{:S(2)}) async-start(), calls=%async_computation.10 | async-start | bytes 524288
  56.7 6.4 copy-start.23
  56.7 8.0 copy-start.22
  63.1 4.2 copy-start.17
  64.9 2.4 copy-start.2
  67.4 14.5 %copy-start.9 = (bf16[256,8192]{1,0:T(8,128)(2,1)S(1)}, bf16[256,8192]{1,0:T(8,128)(2,1)}, u32[]{:S(2)}) copy-start(bf16[256,8192]{1,0:T(8,128)(2,1)} %copy.64) | copy-start | bytes 12582916
  81.9 338.3 %copy-start.20 = (bf16[2,256,2,128]{3,1,2,0:T(8,128)(2,1)}, bf16[2,256,2,128]{3,1,2,0:T(8,128)(2,1)S(1)}, u32[]{:S(2)}) copy-start(bf16[2,256,2,128]{3,1,2,0:T(8,128)(2,1)S(1)} %all_gather.23) | copy-start | bytes 786436
  93.1 324.6 %copy-start.11 = (bf16[2,256,2,128]{3,1,2,0:T(8,128)(2,1)}, bf16[2,256,2,128]{3,1,2,0:T(8,128)(2,1)S(1)}, u32[]{:S(2)}) copy-start(bf16[2,256,2,128]{3,1,2,0:T(8,128)(2,1)S(1)} %all_gather.24) | copy-start | bytes 786436
  109.7 2.3 copy-start.18
  417.7 0.8 copy-start.13
  435.7 1.4 copy-start.14
  435.7 1.7 copy-start.15
  440.7 70.3 %reduce-scatter.3.cloned.1.call-start = ((), (), s32[]{:S(2)}) async-start(), calls=%async_computation.3 | async-start | bytes 327680 | tf_op jit(solution)/shard_map/reduce_scatter | solution.py:110
  459.3 164.0 %all-reduce.7.cloned.1.call-start = ((), (), s32[]{:S(2)}) async-start(), calls=%async_computation.4 | async-start | bytes 4194304 | tf_op jit(solution)/shard_map/psum | solution.py:133
  512.0 5.8 copy-start.8
  537.1 143.5 %all-gather.9.cloned.1.call-start = ((), (), s32[]{:S(2)}) async-start(), calls=%async_computation.5 | async-start | bytes 2621440 | tf_op jit(solution)/shard_map/all_gather | solution.py:48
  623.4 2.2 copy-start.6
  627.5 3.4 copy-start.3
  627.5 3.6 copy-start.4
  631.1 3.8 collective-permute-start
  634.9 0.8 copy-start.19
  635.7 61.4 %copy-start.12 = (bf16[2,256,2,128]{3,1,2,0:T(8,128)(2,1)S(1)}, bf16[2,256,2,128]{3,1,2,0:T(8,128)(2,1)}, u32[]{:S(2)}) copy-start(bf16[2,256,2,128]{3,1,2,0:T(8,128)(2,1)} %copy-done.11) | copy-start | bytes 786436
  635.8 125.5 %all-reduce.13.cloned.1.call-start = ((), (), s32[]{:S(2)}) async-start(), calls=%async_computation.11 | async-start | bytes 524288
  697.0 1.9 copy-start.16
  697.1 3.3 copy-start.21
  719.1 69.3 %reduce-scatter.5.cloned.1.call-start = ((), (), s32[]{:S(2)}) async-start(), calls=%async_computation.6 | async-start | bytes 327680 | tf_op jit(solution)/shard_map/reduce_scatter | solution.py:110
  737.3 163.5 %all-reduce.9.cloned.1.call-start = ((), (), s32[]{:S(2)}) async-start(), calls=%async_computation.7 | async-start | bytes 4194304 | tf_op jit(solution)/shard_map/psum | solution.py:133
  789.4 5.8 copy-start.7
  900.8 2.2 copy-start.5
  903.1 1.2 copy-start.10
  904.0 3.4 copy-start.1
Sparse Core Ops, SparseCore 0:
  8.9 48.3 all-gather.10
  58.9 44.4 all-gather.6
  105.3 295.8 all-gather.12
  440.9 43.1 all-reduce.10
  486.7 24.3 reduce-scatter.2
  537.2 86.1 all-reduce.6
  635.9 44.6 all-gather.8
  719.3 41.9 all-reduce.12
  764.1 24.3 reduce-scatter.4
  814.7 86.1 all-reduce.8
where the time goes:
time: 921 us; the launch traced here: 914 us
  waiting for transfers between devices  596 us (65%)
  matrix products  190 us (21%)
  local copies, waits for them, and re-layouts  62 us (7%)
  other arithmetic  29.4 us (3%)
  blocking collectives  20 us (2%)
  between operations  14.8 us (2%)
    all_gather x1, waiting for transfers between devices, on_device(): wo_layer = lax.all_gather(w_out[0], 'dp', axis=1, tiled=True)  285 us
    psum x2, waiting for transfers between devices, layer_grad(): lax.psum(partial_term.astype(jnp.bfloat16), 'tensor').astype(jnp.float32)  172 us
    unnamed x12, waiting for transfers between devices  49.9 us
    all_gather x2, waiting for transfers between devices, layer_grad(): lax.all_gather(own_upstream, 'tensor', axis=2, tiled=True)  44.6 us
    reduce_scatter x2, waiting for transfers between devices, layer_grad(): lax.psum_scatter(key_terms.astype(jnp.bfloat16), 'dp', scatter_dimension=...  40.8 us
    dot_general x1, local copies, waits for them, and re-layouts, layer_grad(): jnp.einsum('bpd,dc->bpc', normed, w_query, preferred_element_type=jnp.flo...  40 us
    dot_general x2, matrix products, layer_grad(): jnp.einsum('bpc,dc->bpd', grad_q, w_query, preferred_element_type=jnp.flo...  38.6 us
    dot_general x2, matrix products, layer_grad(): jnp.einsum('bpd,cd->bpc', g_whole, w_out, preferred_element_type=jnp.floa...  32.7 us
  transfers between devices with their start and end apart: 11, of which 9 were waited for; matrix products, arithmetic and copies ran while one was open for 15% of the time, Pallas kernels for 0%

commit v1 on v0

--- a/solution.py
+++ b/solution.py
@@ -7,6 +7,19 @@
 HD = 128
 EPS = 1e-05
 THETA = 500000.0
+
+
+def _draft_signs(sample, named_axis):
+    num_devices = lax.axis_size(named_axis)
+    xs_all = [sample]
+    for t in tuple(range(1, num_devices)):
+        xs_all.append(
+            lax.ppermute(
+                xs_all[t - 1], named_axis, [(h, (h - 1) % num_devices) for h in range(num_devices)]
+            )
+        )
+    main = jnp.concatenate(xs_all, axis=2)
+    return jnp.roll(main, lax.axis_index(named_axis) * sample.shape[2], axis=2)
 
 
 def passed_along(value, axis, steps):
@@ -45,7 +58,7 @@
     scale = 1.0 / math.sqrt(HD)
     x_whole, g_whole = (
         lax.all_gather(own_input, "tensor", axis=2, tiled=True),
-        lax.all_gather(own_upstream, "tensor", axis=2, tiled=True),
+        _draft_signs(own_upstream, named_axis="tensor"),
     )
     width = x_whole.shape[2]
     x_full = x_whole.astype(jnp.float32)

time: 921 us -> 849 us (0.922)
  waiting for transfers between devices: 596 us -> 507 us
  starting transfers between devices: 2.56 us -> 19.4 us
    all_gather x1, waiting for transfers between devices: 285 us -> 211 us  [on_device(): wo_layer = lax.all_gather(w_out[0], 'dp', axis=1, tiled=True)]
    ppermute x0 -> x6, waiting for transfers between devices: none -> 55.4 us  [_draft_signs(): lax.ppermute(xs_all[t - 1], named_axis, [(h, (h - 1) % num_devices) for h...]
    all_gather x2 -> x0, waiting for transfers between devices: 44.6 us -> none  [layer_grad(): lax.all_gather(own_upstream, 'tensor', axis=2, tiled=True)]
    unnamed x12 -> x10, waiting for transfers between devices: 49.9 us -> 24.6 us
    ppermute x0 -> x6, starting transfers between devices: none -> 17.4 us  [_draft_signs(): lax.ppermute(xs_all[t - 1], named_axis, [(h, (h - 1) % num_devices) for h...]
  transfers between devices with their start and end apart: 11 -> 15, of which waited for: 9 -> 13; matrix products, arithmetic and copies ran while one was open for 15% -> 20% of each run, Pallas kernels for 0% -> 0%
where the time goes in v1:
time: 849 us; the launch traced here: 842 us
  waiting for transfers between devices  507 us (60%)
  matrix products  184 us (22%)
  local copies, waits for them, and re-layouts  58.2 us (7%)
  other arithmetic  34 us (4%)
  blocking collectives  24 us (3%)
  starting transfers between devices  19.4 us (2%)
  between operations  14.9 us (2%)
    all_gather x1, waiting for transfers between devices, on_device(): wo_layer = lax.all_gather(w_out[0], 'dp', axis=1, tiled=True)  211 us
    psum x2, waiting for transfers between devices, layer_grad(): lax.psum(partial_term.astype(jnp.bfloat16), 'tensor').astype(jnp.float32)  173 us
    ppermute x6, waiting for transfers between devices, _draft_signs(): lax.ppermute(xs_all[t - 1], named_axis, [(h, (h - 1) % num_devices) for h...  55.4 us
    reduce_scatter x2, waiting for transfers between devices, layer_grad(): lax.psum_scatter(key_terms.astype(jnp.bfloat16), 'dp', scatter_dimension=...  40.8 us
    dot_general x1, local copies, waits for them, and re-layouts, layer_grad(): jnp.einsum('bpd,dc->bpc', normed, w_query, preferred_element_type=jnp.flo...  40.8 us
    dot_general x2, matrix products, layer_grad(): jnp.einsum('bpc,dc->bpd', grad_q, w_query, preferred_element_type=jnp.flo...  38.5 us
    dot_general x2, matrix products, layer_grad(): jnp.einsum('bpd,cd->bpc', g_whole, w_out, preferred_element_type=jnp.floa...  33.1 us
    dot_general x2, matrix products, layer_grad(): jnp.einsum('bkgpj,bpkgd->bjkd', grad_scores, q_five, preferred_element_ty...  32.7 us
  transfers between devices with their start and end apart: 15, of which 13 were waited for; matrix products, arithmetic and copies ran while one was open for 20% of the time, Pallas kernels for 0%

profile of v1, /device:TPU:0, one launch (start us, length us, event | category | flops | bytes accessed | tf_op | source)
XLA Modules:
  0.0 841.7 jit_solution(9857649494877500619)
XLA Ops:
  8.5 5.1 collective-permute-start
  13.7 40.8 %copy.63 = bf16[2048,8192]{1,0:T(8,128)(2,1)} copy(bf16[2048,8192]{0,1:T(8,128)(2,1)} %bitcast.235) | data formatting | bytes 67108864 | tf_op jit(solution)/shard_map/bpd,dc->bpc/dot_general | solution.py:70
  54.4 6.4 copy.62
  60.9 6.4 copy.64
  69.3 12.6 %collective-permute-done.1 = bf16[2,64,2048]{2,1,0:T(8,128)(2,1)S(1)} collective-permute-done((bf16[2,64,2048]{2,1,0:T(8,128)(2,1)S(1)}, bf16[2,64,2048]{2,1,0:T(8,128)(2,1)S(1)}, u32[]{:S(2)}, u32[]{:S(2)}) %collective-permute-start.1) | collective-permute-done | bytes 524320 | tf_op jit(solution)/shard_map/ppermute | solution.py:17
  81.9 2.2 collective-permute-start.2
  84.4 10.0 %collective-permute-done.2 = bf16[2,64,2048]{2,1,0:T(8,128)(2,1)S(1)} collective-permute-done((bf16[2,64,2048]{2,1,0:T(8,128)(2,1)S(1)}, bf16[2,64,2048]{2,1,0:T(8,128)(2,1)S(1)}, u32[]{:S(2)}, u32[]{:S(2)}) %collective-permute-start.2) | collective-permute-done | bytes 524320 | tf_op jit(solution)/shard_map/ppermute | solution.py:17
  94.4 4.6 fusion.61
  99.0 2.1 fusion.33
  101.2 4.5 fusion.131
  105.9 11.7 %all_gather.16 = bf16[2,256,2,128]{3,1,2,0:T(8,128)(2,1)S(1)} all-gather(bf16[2,64,2,128]{3,1,2,0:T(8,128)(2,1)S(1)} %fusion.127), channel_id=1, replica_groups=mesh['dp'=4,'section'=2,'tensor'=4] {'dp'}, dimensions={1}, use_global_device_ids=true | all-gather | bytes 327680 | tf_op jit(solution)/shard_map/all_gather | solution.py:86
  119.2 12.2 %all_gather.17 = bf16[2,256,2,128]{3,1,2,0:T(8,128)(2,1)S(1)} all-gather(bf16[2,64,2,128]{3,1,2,0:T(8,128)(2,1)S(1)} %convolution_convert_fusion.1), channel_id=1, replica_groups=mesh['dp'=4,'section'=2,'tensor'=4] {'dp'}, dimensions={1}, use_global_device_ids=true | all-gather | bytes 327680 | tf_op jit(solution)/shard_map/all_gather | solution.py:87
  131.4 15.8 %fusion.129 = f32[2,64,16,128]{3,1,2,0:T(8,128)S(1)} fusion(bf16[16,128,8192,1]{2,1,0,3:T(8,128)(2,1)} %bitcast.236, bf16[1,2,64,8192]{3,2,1,0:T(8,128)(2,1)S(1)} %copy-done.2, f32[8192]{0:T(1024)S(1)} %bitcast.253, f32[2,64]{1,0:T(2,128)S(1)} %get-tuple-element.24), kind=kOutput, calls=%fused_computation.161 | convolution fusion | flops 4299161600 | bytes 36733440 | tf_op jit(solution)/shard_map/bpd,dc->bpc/dot_general | solution.py:70
  148.0 2.2 fusion.160
  150.3 2.9 fusion.157
  153.2 211.2 %all-gather.7.cloned.1.call-done = bf16[1,2048,8192]{2,1,0:T(8,128)(2,1)} async-done(((bf16[1,2048,2048]{2,1,0:T(8,128)(2,1)}), bf16[1,2048,8192]{2,1,0:T(8,128)(2,1)}) %all-gather.7.cloned.1.call-update) | async-done | bytes 33554448 | tf_op jit(solution)/shard_map/all_gather | solution.py:160
  364.4 16.4 %fusion.44 = bf16[2,64,2048]{2,1,0:T(8,128)(2,1)S(1)} fusion(bf16[2,64,8192]{2,1,0:T(8,128)(2,1)} %fusion.61, bf16[1,2048,8192]{2,1,0:T(8,128)(2,1)} %all-gather.7.cloned.1.call-done), kind=kOutput, calls=%fused_computation.52 | convolution fusion | flops 4295229440 | bytes 36175872 | tf_op jit(solution)/shard_map/bpd,cd->bpc/dot_general | solution.py:82
  384.5 13.1 %fusion.91 = f32[2,2,128,8,64]{2,4,3,1,0:T(8,128)S(1)} fusion(f32[2,2,256,64,8]{2,3,4,1,0:T(8,128)} %fusion.110, bf16[2,256,2,128]{3,1,2,0:T(8,128)(2,1)} %copy-done.15, f32[2,2,8,64,256]{4,3,2,1,0:T(8,128)} %get-tuple-element.30, f32[2,2,8,64]{3,2,1,0:T(8,128)S(1)} %get-tuple-element.29), kind=kOutput, calls=%fused_computation.116 | convolution fusion | flops 137890048 | bytes 5513216 | tf_op jit(solution)/shard_map/bkgpj,bjkd->bpkgd/dot_general | solution.py:113
  399.5 16.3 %fusion.80 = bf16[2,256,2,128]{3,1,2,0:T(8,128)(2,1)} fusion(bf16[2,64,2,8,128]{4,1,3,2,0:T(8,128)(2,1)} %bitcast.257, f32[2,2,256,64,8]{2,3,4,1,0:T(8,128)} %fusion.110, f32[2,2,8,64,256]{4,3,2,1,0:T(8,128)} %get-tuple-element.30, f32[2,2,8,64]{3,2,1,0:T(8,128)S(1)} %get-tuple-element.29), kind=kOutput, calls=%fused_computation.96 | convolution fusion | flops 138021120 | bytes 4988928 | tf_op jit(solution)/shard_map/bkgpj,bpkgd->bjkd/dot_general | solution.py:116
  416.0 10.0 %all-reduce.11.cloned.1.call-done = bf16[2,256,2,128]{3,2,0,1:T(2,128)(2,1)} async-done(((bf16[2,256,2,128]{3,2,0,1:T(2,128)(2,1)}), bf16[2,256,2,128]{3,2,0,1:T(2,128)(2,1)}) %all-reduce.11.cloned.1.call-update) | async-done | bytes 262160
  427.0 5.8 fusion.38
  432.8 20.3 %reduce-scatter.3.cloned.1.call-done = bf16[2,64,2,128]{3,1,2,0:T(8,128)(2,1)} async-done(((bf16[2,256,2,128]{3,1,2,0:T(8,128)(2,1)}), bf16[2,64,2,128]{3,1,2,0:T(8,128)(2,1)}) %reduce-scatter.3.cloned.1.call-update) | async-done | bytes 65552 | tf_op jit(solution)/shard_map/reduce_scatter | solution.py:123
  454.0 5.7 fusion.42
  459.7 19.2 %fusion.26 = bf16[2,64,8192]{2,1,0:T(8,128)(2,1)} fusion(f32[2,64,8192]{2,1,0:T(8,128)} %fusion.38, f32[2,64,8192]{2,1,0:T(8,128)} %fusion.42, bf16[1,8192,2048]{2,1,0:T(8,128)(2,1)} %param.16, f32[2,64,16,64]{3,1,2,0:T(8,128)} %get-tuple-element.13, f32[2,64,16,64]{3,1,2,0:T(8,128)} %get-tuple-element.12, f32[2,64,16,128]{3,1,2,0:T(8,128)S(1)} %bitcast.242, ...), kind=kOutput, calls=%fused_computation.16 | convolution fusion | flops 4299161600 | bytes 46170112 | tf_op jit(solution)/shard_map/bpc,dc->bpd/dot_general | solution.py:139
  479.0 86.2 %all-reduce.7.cloned.1.call-done = bf16[2,64,8192]{2,1,0:T(8,128)(2,1)} async-done(((bf16[2,64,8192]{2,1,0:T(8,128)(2,1)}), bf16[2,64,8192]{2,1,0:T(8,128)(2,1)}) %all-reduce.7.cloned.1.call-update) | async-done | bytes 2097168 | tf_op jit(solution)/shard_map/psum | solution.py:146
  565.2 2.2 convert_element_type.155
  567.5 1.9 convert_multiply_fusion.1
  569.4 3.4 fusion.158
  574.1 2.5 collective-permute-done.3
  578.2 12.3 %collective-permute-done.4 = bf16[2,64,2048]{2,1,0:T(8,128)(2,1)S(1)} collective-permute-done((bf16[2,64,2048]{2,1,0:T(8,128)(2,1)S(1)}, bf16[2,64,2048]{2,1,0:T(8,128)(2,1)S(1)}, u32[]{:S(2)}, u32[]{:S(2)}) %collective-permute-start.4) | collective-permute-done | bytes 524320 | tf_op jit(solution)/shard_map/ppermute | solution.py:17
  590.6 3.4 collective-permute-start.5
  594.0 10.6 %collective-permute-done.5 = bf16[2,64,2048]{2,1,0:T(8,128)(2,1)S(1)} collective-permute-done((bf16[2,64,2048]{2,1,0:T(8,128)(2,1)S(1)}, bf16[2,64,2048]{2,1,0:T(8,128)(2,1)S(1)}, u32[]{:S(2)}, u32[]{:S(2)}) %collective-permute-start.5) | collective-permute-done | bytes 524320 | tf_op jit(solution)/shard_map/ppermute | solution.py:17
  604.6 4.5 collective-permute-start.6
  609.1 9.8 %collective-permute-done.6 = bf16[2,64,2048]{2,1,0:T(8,128)(2,1)S(1)} collective-permute-done((bf16[2,64,2048]{2,1,0:T(8,128)(2,1)S(1)}, bf16[2,64,2048]{2,1,0:T(8,128)(2,1)S(1)}, u32[]{:S(2)}, u32[]{:S(2)}) %collective-permute-start.6) | collective-permute-done | bytes 524320 | tf_op jit(solution)/shard_map/ppermute | solution.py:17
  618.8 3.7 fusion.54
  622.6 16.7 %fusion.47 = bf16[2,64,2048]{2,1,0:T(8,128)(2,1)S(1)} fusion(bf16[2,64,8192]{2,1,0:T(8,128)(2,1)S(1)} %fusion.54, bf16[1,2048,8192]{2,1,0:T(8,128)(2,1)} %all-gather.7.cloned.1.call-done), kind=kOutput, calls=%fused_computation.53 | convolution fusion | flops 4295229440 | bytes 36175872 | tf_op jit(solution)/shard_map/bpd,cd->bpc/dot_general | solution.py:82
  639.4 2.0 fusion.77
  641.5 1.8 fusion.107
  644.2 13.3 %fusion.93 = f32[2,2,128,8,64]{2,4,3,1,0:T(8,128)S(1)} fusion(f32[2,2,256,64,8]{2,3,4,1,0:T(8,128)} %fusion.107, bf16[2,256,2,128]{3,1,2,0:T(8,128)(2,1)} %copy-done.15, f32[2,2,8,64,256]{4,3,2,1,0:T(8,128)} %get-tuple-element.30, f32[2,2,8,64]{3,2,1,0:T(8,128)S(1)} %get-tuple-element.29), kind=kOutput, calls=%fused_computation.118 | convolution fusion | flops 137890048 | bytes 5513216 | tf_op jit(solution)/shard_map/bkgpj,bjkd->bpkgd/dot_general | solution.py:113
  659.3 16.4 %fusion.78 = bf16[2,256,2,128]{3,1,2,0:T(8,128)(2,1)} fusion(bf16[2,64,2,8,128]{4,1,3,2,0:T(8,128)(2,1)} %bitcast.258, f32[2,2,256,64,8]{2,3,4,1,0:T(8,128)} %fusion.107, f32[2,2,8,64,256]{4,3,2,1,0:T(8,128)} %get-tuple-element.30, f32[2,2,8,64]{3,2,1,0:T(8,128)S(1)} %get-tuple-element.29), kind=kOutput, calls=%fused_computation.94 | convolution fusion | flops 138021120 | bytes 4988928 | tf_op jit(solution)/shard_map/bkgpj,bpkgd->bjkd/dot_general | solution.py:116
  676.0 13.0 %all-reduce.13.cloned.1.call-done = bf16[2,256,2,128]{3,2,0,1:T(2,128)(2,1)} async-done(((bf16[2,256,2,128]{3,2,0,1:T(2,128)(2,1)}), bf16[2,256,2,128]{3,2,0,1:T(2,128)(2,1)}) %all-reduce.13.cloned.1.call-update) | async-done | bytes 262160
  690.0 5.6 fusion.36
  695.6 20.5 %reduce-scatter.5.cloned.1.call-done = bf16[2,64,2,128]{3,1,2,0:T(8,128)(2,1)} async-done(((bf16[2,256,2,128]{3,1,2,0:T(8,128)(2,1)}), bf16[2,64,2,128]{3,1,2,0:T(8,128)(2,1)}) %reduce-scatter.5.cloned.1.call-update) | async-done | bytes 65552 | tf_op jit(solution)/shard_map/reduce_scatter | solution.py:123
  717.1 5.7 fusion.40
  722.8 19.2 %fusion.23 = bf16[2,64,8192]{2,1,0:T(8,128)(2,1)} fusion(f32[2,64,8192]{2,1,0:T(8,128)} %fusion.36, f32[2,64,8192]{2,1,0:T(8,128)} %fusion.40, bf16[1,8192,2048]{2,1,0:T(8,128)(2,1)} %param.16, f32[2,64,16,64]{3,1,2,0:T(8,128)} %get-tuple-element.11, f32[2,64,16,64]{3,1,2,0:T(8,128)} %get-tuple-element.10, f32[2,64,16,128]{3,1,2,0:T(8,128)S(1)} %bitcast.240, ...), kind=kOutput, calls=%fused_computation.15 | convolution fusion | flops 4299161600 | bytes 46170112 | tf_op jit(solution)/shard_map/bpc,dc->bpd/dot_general | solution.py:139
  742.1 86.3 %all-reduce.9.cloned.1.call-done = bf16[2,64,8192]{2,1,0:T(8,128)(2,1)} async-done(((bf16[2,64,8192]{2,1,0:T(8,128)(2,1)}), bf16[2,64,8192]{2,1,0:T(8,128)(2,1)}) %all-reduce.9.cloned.1.call-update) | async-done | bytes 2097168 | tf_op jit(solution)/shard_map/psum | solution.py:146
  828.4 2.2 convert_element_type.169
  831.5 3.1 fusion.84
  (95 shorter events, 22.6 us)
Async XLA Ops:
  6.5 1.5 copy-start
  6.5 92.5 %all-gather.5.cloned.1.call-start = ((), (), s32[]{:S(2)}) async-start(), calls=%async_computation.6 | async-start | bytes 2621440 | tf_op jit(solution)/shard_map/all_gather | solution.py:60
  7.3 0.8 copy-start.16
  7.3 357.1 %all-gather.7.cloned.1.call-start = ((), (), s32[]{:S(2)}) async-start(), calls=%async_computation.7 | async-start | bytes 41943040 | tf_op jit(solution)/shard_map/all_gather | solution.py:160
  8.0 418.0 %all-reduce.11.cloned.1.call-start = ((), (), s32[]{:S(2)}) async-start(), calls=%async_computation.8 | async-start | bytes 524288
  8.5 60.0 %collective-permute-start = (bf16[2,64,2048]{2,1,0:T(8,128)(2,1)S(1)}, bf16[2,64,2048]{2,1,0:T(8,128)(2,1)S(1)}, u32[]{:S(2)}, u32[]{:S(2)}) collective-permute-start(bf16[2,64,2048]{2,1,0:T(8,128)(2,1)S(1)} %fusion.50), channel_id=1, source_target_pairs={{0,3},{1,0},{2,1},{3,2},{4,7},{5,4},{6,5},{7,6},{8,11},{9,8},{10,9... | collective-permute-start | bytes 1572872 | tf_op jit(solution)/shard_map/ppermute | solution.py:17
  60.9 6.4 copy-start.18
  60.9 7.7 copy-start.17
  67.2 33.9 %copy-start.13 = (f32[1,8192]{1,0:T(1,128)S(1)}, f32[1,8192]{1,0:T(1,128)}, u32[]{:S(2)}) copy-start(f32[1,8192]{1,0:T(1,128)} %param.15) | copy-start | bytes 98308
  68.5 13.4 %collective-permute-start.1 = (bf16[2,64,2048]{2,1,0:T(8,128)(2,1)S(1)}, bf16[2,64,2048]{2,1,0:T(8,128)(2,1)S(1)}, u32[]{:S(2)}, u32[]{:S(2)}) collective-permute-start(bf16[2,64,2048]{2,1,0:T(8,128)(2,1)S(1)} %collective-permute-done), channel_id=1, source_target_pairs={{0,3},{1,0},{2,1},{3,2},{4,7},{5,4},{6,5},{7,6},{8,11},{9,8},{10,9... | collective-permute-start | bytes 1572872 | tf_op jit(solution)/shard_map/ppermute | solution.py:17
  81.9 12.5 %collective-permute-start.2 = (bf16[2,64,2048]{2,1,0:T(8,128)(2,1)S(1)}, bf16[2,64,2048]{2,1,0:T(8,128)(2,1)S(1)}, u32[]{:S(2)}, u32[]{:S(2)}) collective-permute-start(bf16[2,64,2048]{2,1,0:T(8,128)(2,1)S(1)} %collective-permute-done.1), channel_id=1, source_target_pairs={{0,3},{1,0},{2,1},{3,2},{4,7},{5,4},{6,5},{7,6},{8,11},{9,8},{10,9... | collective-permute-start | bytes 1572872 | tf_op jit(solution)/shard_map/ppermute | solution.py:17
  101.1 16.5 %copy-start.2 = (bf16[1,2,64,8192]{3,2,1,0:T(8,128)(2,1)S(1)}, bf16[1,2,64,8192]{3,2,1,0:T(8,128)(2,1)}, u32[]{:S(2)}) copy-start(bf16[1,2,64,8192]{3,2,1,0:T(8,128)(2,1)} %all-gather.5.cloned.1.call-done) | copy-start | bytes 6291460
  101.2 16.5 %copy-start.8 = (bf16[256,8192]{1,0:T(8,128)(2,1)S(1)}, bf16[256,8192]{1,0:T(8,128)(2,1)}, u32[]{:S(2)}) copy-start(bf16[256,8192]{1,0:T(8,128)(2,1)} %copy.64) | copy-start | bytes 12582916
  117.6 30.4 %copy-start.15 = (bf16[2,256,2,128]{3,1,2,0:T(8,128)(2,1)}, bf16[2,256,2,128]{3,1,2,0:T(8,128)(2,1)S(1)}, u32[]{:S(2)}) copy-start(bf16[2,256,2,128]{3,1,2,0:T(8,128)(2,1)S(1)} %all_gather.16) | copy-start | bytes 786436
  131.4 251.3 %copy-start.10 = (bf16[2,256,2,128]{3,1,2,0:T(8,128)(2,1)}, bf16[2,256,2,128]{3,1,2,0:T(8,128)(2,1)S(1)}, u32[]{:S(2)}) copy-start(bf16[2,256,2,128]{3,1,2,0:T(8,128)(2,1)S(1)} %all_gather.17) | copy-start | bytes 786436
  148.0 232.8 %copy-start.14 = (bf16[2,64,16,128]{3,1,2,0:T(8,128)(2,1)}, bf16[2,64,16,128]{3,1,2,0:T(8,128)(2,1)S(1)}, u32[]{:S(2)}) copy-start(bf16[2,64,16,128]{3,1,2,0:T(8,128)(2,1)S(1)} %fusion.88) | copy-start | bytes 1572868
  364.4 16.6 %copy-start.12 = (bf16[2,2,8,64,256]{4,3,2,1,0:T(8,128)(2,1)S(1)}, bf16[2,2,8,64,256]{4,3,2,1,0:T(8,128)(2,1)}, u32[]{:S(2)}) copy-start(bf16[2,2,8,64,256]{4,3,2,1,0:T(8,128)(2,1)} %fusion.157) | copy-start | bytes 3145732
  382.7 70.3 %reduce-scatter.3.cloned.1.call-start = ((), (), s32[]{:S(2)}) async-start(), calls=%async_computation.2 | async-start | bytes 327680 | tf_op jit(solution)/shard_map/reduce_scatter | solution.py:123
  415.8 149.4 %all-reduce.7.cloned.1.call-start = ((), (), s32[]{:S(2)}) async-start(), calls=%async_computation.3 | async-start | bytes 4194304 | tf_op jit(solution)/shard_map/psum | solution.py:146
  478.9 210.1 %all-reduce.13.cloned.1.call-start = ((), (), s32[]{:S(2)}) async-start(), calls=%async_computation.9 | async-start | bytes 524288
  565.2 2.2 copy-start.7
  569.4 39.7 %copy-start.4 = (f32[2,64,8192]{2,1,0:T(8,128)}, f32[2,64,8192]{2,1,0:T(8,128)S(1)}, u32[]{:S(2)}) copy-start(f32[2,64,8192]{2,1,0:T(8,128)S(1)} %get-tuple-element.8) | copy-start | bytes 12582916
  569.4 49.4 %copy-start.5 = (f32[2,64,8192]{2,1,0:T(8,128)}, f32[2,64,8192]{2,1,0:T(8,128)S(1)}, u32[]{:S(2)}) copy-start(f32[2,64,8192]{2,1,0:T(8,128)S(1)} %get-tuple-element.22) | copy-start | bytes 12582916
  572.8 3.8 collective-permute-start.3
  576.6 14.0 %collective-permute-start.4 = (bf16[2,64,2048]{2,1,0:T(8,128)(2,1)S(1)}, bf16[2,64,2048]{2,1,0:T(8,128)(2,1)S(1)}, u32[]{:S(2)}, u32[]{:S(2)}) collective-permute-start(bf16[2,64,2048]{2,1,0:T(8,128)(2,1)S(1)} %collective-permute-done.3), channel_id=1, source_target_pairs={{0,3},{1,0},{2,1},{3,2},{4,7},{5,4},{6,5},{7,6},{8,11},{9,8},{10,9... | collective-permute-start | bytes 1572872 | tf_op jit(solution)/shard_map/ppermute | solution.py:17
  590.6 14.0 %collective-permute-start.5 = (bf16[2,64,2048]{2,1,0:T(8,128)(2,1)S(1)}, bf16[2,64,2048]{2,1,0:T(8,128)(2,1)S(1)}, u32[]{:S(2)}, u32[]{:S(2)}) collective-permute-start(bf16[2,64,2048]{2,1,0:T(8,128)(2,1)S(1)} %collective-permute-done.4), channel_id=1, source_target_pairs={{0,3},{1,0},{2,1},{3,2},{4,7},{5,4},{6,5},{7,6},{8,11},{9,8},{10,9... | collective-permute-start | bytes 1572872 | tf_op jit(solution)/shard_map/ppermute | solution.py:17
  604.6 14.2 %collective-permute-start.6 = (bf16[2,64,2048]{2,1,0:T(8,128)(2,1)S(1)}, bf16[2,64,2048]{2,1,0:T(8,128)(2,1)S(1)}, u32[]{:S(2)}, u32[]{:S(2)}) collective-permute-start(bf16[2,64,2048]{2,1,0:T(8,128)(2,1)S(1)} %collective-permute-done.5), channel_id=1, source_target_pairs={{0,3},{1,0},{2,1},{3,2},{4,7},{5,4},{6,5},{7,6},{8,11},{9,8},{10,9... | collective-permute-start | bytes 1572872 | tf_op jit(solution)/shard_map/ppermute | solution.py:17
  622.6 16.7 %copy-start.3 = (bf16[2,64,8192]{2,1,0:T(8,128)(2,1)}, bf16[2,64,8192]{2,1,0:T(8,128)(2,1)S(1)}, u32[]{:S(2)}) copy-start(bf16[2,64,8192]{2,1,0:T(8,128)(2,1)S(1)} %fusion.54) | copy-start | bytes 6291460
  622.6 18.9 %copy-start.11 = (bf16[2,256,2,128]{3,1,2,0:T(8,128)(2,1)S(1)}, bf16[2,256,2,128]{3,1,2,0:T(8,128)(2,1)}, u32[]{:S(2)}) copy-start(bf16[2,256,2,128]{3,1,2,0:T(8,128)(2,1)} %copy-done.10) | copy-start | bytes 786436
  644.1 72.0 %reduce-scatter.5.cloned.1.call-start = ((), (), s32[]{:S(2)}) async-start(), calls=%async_computation.4 | async-start | bytes 327680 | tf_op jit(solution)/shard_map/reduce_scatter | solution.py:123
  675.7 152.7 %all-reduce.9.cloned.1.call-start = ((), (), s32[]{:S(2)}) async-start(), calls=%async_computation.5 | async-start | bytes 4194304 | tf_op jit(solution)/shard_map/psum | solution.py:146
  742.1 89.4 %copy-start.9 = (f32[2,64,2048]{2,1,0:T(8,128)S(1)}, f32[2,64,2048]{2,1,0:T(8,128)}, u32[]{:S(2)}) copy-start(f32[2,64,2048]{2,1,0:T(8,128)} %get-tuple-element.7) | copy-start | bytes 3145732
  828.4 2.2 copy-start.6
  828.4 6.2 copy-start.1
Sparse Core Ops, SparseCore 0:
  8.9 50.2 all-gather.4
  61.0 303.3 all-gather.6
  382.8 43.2 all-reduce.10
  428.7 24.3 reduce-scatter.2
  479.1 86.1 all-reduce.6
  644.3 44.7 all-reduce.12
  691.8 24.3 reduce-scatter.4
  742.2 86.1 all-reduce.8
